TPU v7x, 32 devices: a whole 2x2x4 slice. The times are simulated.
32 devices in a mesh: segment: 4 (over y, x), col: 8 (over z, core).
Axes of the slice: x: 2, y: 2, z: 4, core: 2. Of those that a mesh axis runs over, the one named last changes fastest.
Arguments:
- left_env: bfloat16 [384, 8192], P(None, 'col'), may hold values from -6 to 6
- bit_strings: int32 [384, 4], P(None, 'segment'), may hold values from 0 to 1
- site_tensors: bfloat16 [4, 2, 8192, 8192], P('segment', None, None, 'col'), may hold values from -0.0625 to 0.0625
Outputs:
- section_env: bfloat16 [4, 384, 8192], P('segment', None, 'col')
- section_log: float32 [4, 384], P('segment')
All inputs are finite; a program needn't handle non-finite values. Where the computation divides by a largest or mean magnitude, that divisor is 1e-20 or more.
Results may differ from a plain program's by a relative error of at most 0.0065.
Values may be sent and summed in bfloat16 or wider, within the bound.
A program may use at most 128 MiB of HBM per device.

v0:
```python
import jax
import jax.numpy as jnp
from jax import lax
from jax.sharding import PartitionSpec as P

MICRO = 2


epsilon = 1e-06


def passed_along(value, axis, by):
    length = lax.axis_size(axis)
    pairs = [(i, i + by) for i in range(length) if 0 <= i + by < length]
    return lax.ppermute(value, axis, pairs)


def advance(vector, bit_column, tensor):
    batch_rows = vector.shape[0]
    col_width = tensor.shape[2]
    block = min(128, batch_rows)
    buffer_rows = (batch_rows + block - 1 + block - 1) // block * block
    block_count = buffer_rows // block
    ones_before = jnp.cumsum(bit_column) - bit_column
    index_rows = jnp.arange(batch_rows, dtype=jnp.int32)
    zeros_before = index_rows - ones_before
    zero_count = batch_rows - jnp.sum(bit_column)
    start_one = (zero_count + block - 1) // block * block
    slot = jnp.where(bit_column == 1, start_one + ones_before, zeros_before)
    source = jnp.zeros((buffer_rows,), jnp.int32).at[slot].set(index_rows)
    filled = jnp.zeros((buffer_rows,), jnp.bool_).at[slot].set(True)
    block_bit = (jnp.arange(block_count, dtype=jnp.int32) * block >= start_one).astype(jnp.int32)
    arranged_in = jnp.where(
        filled[:, None], jnp.take(vector, source, axis=0), jnp.zeros((), vector.dtype)
    )
    gathered_piece = lax.all_gather(arranged_in, "col", axis=1, tiled=True)
    width = gathered_piece.shape[1]
    pieces = gathered_piece.reshape(block_count, block, width)

    def one_block(inputs):
        rows_block, bit_value = inputs
        weight_block = lax.dynamic_slice(
            tensor, (bit_value, 0, jnp.int32(0)), (1, width, col_width)
        )[0]
        return jnp.dot(rows_block, weight_block, preferred_element_type=jnp.float32)

    result = lax.map(one_block, (pieces, block_bit))
    arranged_out = result.reshape(buffer_rows, col_width)
    chosen = jnp.take(arranged_out, slot, axis=0)
    maximum = lax.pmax(jnp.max(jnp.abs(chosen), axis=1), "col") + epsilon
    return ((chosen / maximum[:, None]).astype(jnp.bfloat16), jnp.log(maximum))


def local(left_env, bit_strings, site_tensors):
    segment_count = lax.axis_size("segment")
    segment_index = lax.axis_index("segment")
    row_count = left_env.shape[0]
    col_width = left_env.shape[1]
    granules = 2 * MICRO
    batch_rows = row_count // granules
    env_out = jnp.zeros((row_count, col_width), jnp.bfloat16)
    log_out = jnp.zeros((row_count,), jnp.float32)
    incoming = jnp.zeros((batch_rows, col_width), jnp.bfloat16)
    tick_total = granules + segment_count - 1
    for tick_step in range(tick_total):
        position = tick_step - segment_index
        active = (position >= 0) & (position < granules)
        offset_rows = jnp.clip(position, 0, granules - 1) * batch_rows
        from_input = lax.dynamic_slice_in_dim(left_env, offset_rows, batch_rows, 0)
        current = jnp.where(segment_index == 0, from_input, incoming)
        bit_block = lax.dynamic_slice_in_dim(bit_strings, offset_rows, batch_rows, 0)
        current, logs_site = advance(current, bit_block[:, 0], site_tensors[0])
        old_env = lax.dynamic_slice_in_dim(env_out, offset_rows, batch_rows, 0)
        old_log = lax.dynamic_slice_in_dim(log_out, offset_rows, batch_rows, 0)
        env_out = lax.dynamic_update_slice_in_dim(
            env_out, jnp.where(active, current, old_env), offset_rows, 0
        )
        log_out = lax.dynamic_update_slice_in_dim(
            log_out, jnp.where(active, logs_site, old_log), offset_rows, 0
        )
        if tick_step + 1 < tick_total:
            incoming = passed_along(current, "segment", 1)
    return (env_out[None], log_out[None])


def solution(mesh):
    placed = (P(None, "col"), P(None, "segment"), P("segment", None, None, "col"))
    return jax.shard_map(
        local,
        mesh=mesh,
        in_specs=placed,
        out_specs=(P("segment", None, "col"), P("segment", None)),
        check_vma=False,
    )
```

profile of v0, /device:TPU:31, one launch (start us, length us, event | category | flops | bytes accessed | tf_op | source)
XLA Modules:
  0.0 609.9 jit_solution(9324668334376139181)
XLA Ops:
  7.2 1.8 fusion.162
  17.9 34.6 %all-gather.8.cloned.1.call-done = bf16[192,8192]{1,0:T(8,128)(2,1)} async-done(((bf16[192,1024]{1,0:T(8,128)(2,1)}), bf16[192,8192]{1,0:T(8,128)(2,1)}) %all-gather.8.cloned.1.call-update) | async-done | bytes 3145744 | tf_op jit(solution)/shard_map/all_gather | solution.py:36
  52.5 23.1 %while.70 = (s32[]{:T(128)}, f32[2,96,1024]{2,1,0:T(8,128)S(1)}, bf16[2,96,8192]{2,1,0:T(8,128)(2,1)}, s32[2]{0:T(128)S(1)}, bf16[2,8192,1024]{2,1,0:T(8,128)(2,1)}, /*index=5*/s32[]{:T(128)}, s32[]{:T(128)}, s32[]{:T(128)}) while((s32[]{:T(128)}, f32[2,96,1024]{2,1,0:T(8,128)S(1)}, bf16[2,96,8192]{2,1,0:T(8,128)(2,1)}, s32[2]{0:T(128)S(1)}, ...), condition=%wide.region_5.7_spmd, body=%wide.region_4.6_spmd.sunk | while | flops 1610612736 | bytes 18744456 | solution.py:47
  55.1 9.0 %fusion.192 = f32[2,96,1024]{2,1,0:T(8,128)S(1)} fusion(f32[2,96,1024]{2,1,0:T(8,128)S(1)} %get-tuple-element.582, s32[]{:T(128)} %get-tuple-element.581, bf16[2,8192,1024]{2,1,0:T(8,128)(2,1)} %get-tuple-element.593, s32[]{:T(128)S(6)} %select_n.653, bf16[2,96,8192]{2,1,0:T(8,128)(2,1)} %get-tuple-element.591), kind=kOutput, calls=%fused_computation.34.clone.1 | convolution fusion | flops 1610612736 | bytes 18744324 | tf_op jit(solution)/shard_map/while/body/eval_jaxpr/dot_general | solution.py:45
  66.7 9.0 %fusion.192 = f32[2,96,1024]{2,1,0:T(8,128)S(1)} fusion(f32[2,96,1024]{2,1,0:T(8,128)S(1)} %get-tuple-element.582, s32[]{:T(128)} %get-tuple-element.581, bf16[2,8192,1024]{2,1,0:T(8,128)(2,1)} %get-tuple-element.593, s32[]{:T(128)S(6)} %select_n.653, bf16[2,96,8192]{2,1,0:T(8,128)(2,1)} %get-tuple-element.591), kind=kOutput, calls=%fused_computation.34.clone.1 | convolution fusion | flops 1610612736 | bytes 18744324 | tf_op jit(solution)/shard_map/while/body/eval_jaxpr/dot_general | solution.py:45
  76.6 13.1 %pmax.49 = f32[96]{0:T(128)S(1)} all-reduce(f32[96]{0:T(128)S(1)} %abs_reduce_fusion.6), channel_id=1, replica_groups=mesh['segment'=4,'col'=8] {'col'}, use_global_device_ids=true, to_apply=%region_7.10 | all-reduce | flops 96 | bytes 768 | tf_op jit(solution)/shard_map/pmax | solution.py:50
  90.0 1.3 collective-permute-start
  91.3 6.4 %collective-permute-done = bf16[96,1024]{1,0:T(8,128)(2,1)S(1)} collective-permute-done((bf16[96,1024]{1,0:T(8,128)(2,1)S(1)}, bf16[96,1024]{1,0:T(8,128)(2,1)S(1)}, u32[]{:S(2)}, u32[]{:S(2)}) %collective-permute-start) | collective-permute-done | bytes 196640 | tf_op jit(solution)/shard_map/ppermute | solution.py:15
  102.9 34.9 %all-gather.10.cloned.1.call-done = bf16[192,8192]{1,0:T(8,128)(2,1)} async-done(((bf16[192,1024]{1,0:T(8,128)(2,1)}), bf16[192,8192]{1,0:T(8,128)(2,1)}) %all-gather.10.cloned.1.call-update) | async-done | bytes 3145744 | tf_op jit(solution)/shard_map/all_gather | solution.py:36
  137.9 23.1 %while.71 = (s32[]{:T(128)}, f32[2,96,1024]{2,1,0:T(8,128)S(1)}, bf16[2,96,8192]{2,1,0:T(8,128)(2,1)}, s32[2]{0:T(128)S(1)}, bf16[2,8192,1024]{2,1,0:T(8,128)(2,1)}, /*index=5*/s32[]{:T(128)}, s32[]{:T(128)}, s32[]{:T(128)}) while((s32[]{:T(128)}, f32[2,96,1024]{2,1,0:T(8,128)S(1)}, bf16[2,96,8192]{2,1,0:T(8,128)(2,1)}, s32[2]{0:T(128)S(1)}, ...), condition=%wide.region_13.16_spmd, body=%wide.region_12.15_spmd.sunk | while | flops 1610612736 | bytes 18744456 | solution.py:47
  140.4 9.0 %fusion.195 = f32[2,96,1024]{2,1,0:T(8,128)S(1)} fusion(f32[2,96,1024]{2,1,0:T(8,128)S(1)} %get-tuple-element.606, s32[]{:T(128)} %get-tuple-element.605, bf16[2,8192,1024]{2,1,0:T(8,128)(2,1)} %get-tuple-element.617, s32[]{:T(128)S(6)} %select_n.654, bf16[2,96,8192]{2,1,0:T(8,128)(2,1)} %get-tuple-element.615), kind=kOutput, calls=%fused_computation.42.clone.1 | convolution fusion | flops 1610612736 | bytes 18744324 | tf_op jit(solution)/shard_map/while/body/eval_jaxpr/dot_general | solution.py:45
  152.0 9.0 %fusion.195 = f32[2,96,1024]{2,1,0:T(8,128)S(1)} fusion(f32[2,96,1024]{2,1,0:T(8,128)S(1)} %get-tuple-element.606, s32[]{:T(128)} %get-tuple-element.605, bf16[2,8192,1024]{2,1,0:T(8,128)(2,1)} %get-tuple-element.617, s32[]{:T(128)S(6)} %select_n.654, bf16[2,96,8192]{2,1,0:T(8,128)(2,1)} %get-tuple-element.615), kind=kOutput, calls=%fused_computation.42.clone.1 | convolution fusion | flops 1610612736 | bytes 18744324 | tf_op jit(solution)/shard_map/while/body/eval_jaxpr/dot_general | solution.py:45
  161.9 13.1 %pmax.50 = f32[96]{0:T(128)S(1)} all-reduce(f32[96]{0:T(128)S(1)} %abs_reduce_fusion.5), channel_id=1, replica_groups=mesh['segment'=4,'col'=8] {'col'}, use_global_device_ids=true, to_apply=%region_15.18 | all-reduce | flops 96 | bytes 768 | tf_op jit(solution)/shard_map/pmax | solution.py:50
  175.3 1.5 collective-permute-start.1
  176.8 6.3 %collective-permute-done.1 = bf16[96,1024]{1,0:T(8,128)(2,1)S(1)} collective-permute-done((bf16[96,1024]{1,0:T(8,128)(2,1)S(1)}, bf16[96,1024]{1,0:T(8,128)(2,1)S(1)}, u32[]{:S(2)}, u32[]{:S(2)}) %collective-permute-start.1) | collective-permute-done | bytes 196640 | tf_op jit(solution)/shard_map/ppermute | solution.py:15
  187.9 35.1 %all-gather.12.cloned.1.call-done = bf16[192,8192]{1,0:T(8,128)(2,1)} async-done(((bf16[192,1024]{1,0:T(8,128)(2,1)}), bf16[192,8192]{1,0:T(8,128)(2,1)}) %all-gather.12.cloned.1.call-update) | async-done | bytes 3145744 | tf_op jit(solution)/shard_map/all_gather | solution.py:36
  223.1 23.1 %while.72 = (s32[]{:T(128)}, f32[2,96,1024]{2,1,0:T(8,128)S(1)}, bf16[2,96,8192]{2,1,0:T(8,128)(2,1)}, s32[2]{0:T(128)S(1)}, bf16[2,8192,1024]{2,1,0:T(8,128)(2,1)}, /*index=5*/s32[]{:T(128)}, s32[]{:T(128)}, s32[]{:T(128)}) while((s32[]{:T(128)}, f32[2,96,1024]{2,1,0:T(8,128)S(1)}, bf16[2,96,8192]{2,1,0:T(8,128)(2,1)}, s32[2]{0:T(128)S(1)}, ...), condition=%wide.region_21.24_spmd, body=%wide.region_20.23_spmd.sunk | while | flops 1610612736 | bytes 18744456 | solution.py:47
  225.7 9.0 %fusion.198 = f32[2,96,1024]{2,1,0:T(8,128)S(1)} fusion(f32[2,96,1024]{2,1,0:T(8,128)S(1)} %get-tuple-element.630, s32[]{:T(128)} %get-tuple-element.629, bf16[2,8192,1024]{2,1,0:T(8,128)(2,1)} %get-tuple-element.641, s32[]{:T(128)S(6)} %select_n.655, bf16[2,96,8192]{2,1,0:T(8,128)(2,1)} %get-tuple-element.639), kind=kOutput, calls=%fused_computation.50.clone.1 | convolution fusion | flops 1610612736 | bytes 18744324 | tf_op jit(solution)/shard_map/while/body/eval_jaxpr/dot_general | solution.py:45
  237.2 9.0 %fusion.198 = f32[2,96,1024]{2,1,0:T(8,128)S(1)} fusion(f32[2,96,1024]{2,1,0:T(8,128)S(1)} %get-tuple-element.630, s32[]{:T(128)} %get-tuple-element.629, bf16[2,8192,1024]{2,1,0:T(8,128)(2,1)} %get-tuple-element.641, s32[]{:T(128)S(6)} %select_n.655, bf16[2,96,8192]{2,1,0:T(8,128)(2,1)} %get-tuple-element.639), kind=kOutput, calls=%fused_computation.50.clone.1 | convolution fusion | flops 1610612736 | bytes 18744324 | tf_op jit(solution)/shard_map/while/body/eval_jaxpr/dot_general | solution.py:45
  247.2 13.1 %pmax.51 = f32[96]{0:T(128)S(1)} all-reduce(f32[96]{0:T(128)S(1)} %abs_reduce_fusion.4), channel_id=1, replica_groups=mesh['segment'=4,'col'=8] {'col'}, use_global_device_ids=true, to_apply=%region_23.26 | all-reduce | flops 96 | bytes 768 | tf_op jit(solution)/shard_map/pmax | solution.py:50
  260.6 1.3 collective-permute-start.2
  261.9 6.5 %collective-permute-done.2 = bf16[96,1024]{1,0:T(8,128)(2,1)S(1)} collective-permute-done((bf16[96,1024]{1,0:T(8,128)(2,1)S(1)}, bf16[96,1024]{1,0:T(8,128)(2,1)S(1)}, u32[]{:S(2)}, u32[]{:S(2)}) %collective-permute-start.2) | collective-permute-done | bytes 196640 | tf_op jit(solution)/shard_map/ppermute | solution.py:15
  273.5 34.8 %all-gather.14.cloned.1.call-done = bf16[192,8192]{1,0:T(8,128)(2,1)} async-done(((bf16[192,1024]{1,0:T(8,128)(2,1)}), bf16[192,8192]{1,0:T(8,128)(2,1)}) %all-gather.14.cloned.1.call-update) | async-done | bytes 3145744 | tf_op jit(solution)/shard_map/all_gather | solution.py:36
  308.4 23.1 %while.73 = (s32[]{:T(128)}, f32[2,96,1024]{2,1,0:T(8,128)S(1)}, bf16[2,96,8192]{2,1,0:T(8,128)(2,1)}, s32[2]{0:T(128)S(1)}, bf16[2,8192,1024]{2,1,0:T(8,128)(2,1)}, /*index=5*/s32[]{:T(128)}, s32[]{:T(128)}, s32[]{:T(128)}) while((s32[]{:T(128)}, f32[2,96,1024]{2,1,0:T(8,128)S(1)}, bf16[2,96,8192]{2,1,0:T(8,128)(2,1)}, s32[2]{0:T(128)S(1)}, ...), condition=%wide.region_29.32_spmd, body=%wide.region_28.31_spmd.sunk | while | flops 1610612736 | bytes 18744456 | solution.py:47
  310.9 9.0 %fusion.201 = f32[2,96,1024]{2,1,0:T(8,128)S(1)} fusion(f32[2,96,1024]{2,1,0:T(8,128)S(1)} %get-tuple-element.654, s32[]{:T(128)} %get-tuple-element.653, bf16[2,8192,1024]{2,1,0:T(8,128)(2,1)} %get-tuple-element.665, s32[]{:T(128)S(6)} %select_n.656, bf16[2,96,8192]{2,1,0:T(8,128)(2,1)} %get-tuple-element.663), kind=kOutput, calls=%fused_computation.58.clone.1 | convolution fusion | flops 1610612736 | bytes 18744324 | tf_op jit(solution)/shard_map/while/body/eval_jaxpr/dot_general | solution.py:45
  322.5 9.0 %fusion.201 = f32[2,96,1024]{2,1,0:T(8,128)S(1)} fusion(f32[2,96,1024]{2,1,0:T(8,128)S(1)} %get-tuple-element.654, s32[]{:T(128)} %get-tuple-element.653, bf16[2,8192,1024]{2,1,0:T(8,128)(2,1)} %get-tuple-element.665, s32[]{:T(128)S(6)} %select_n.656, bf16[2,96,8192]{2,1,0:T(8,128)(2,1)} %get-tuple-element.663), kind=kOutput, calls=%fused_computation.58.clone.1 | convolution fusion | flops 1610612736 | bytes 18744324 | tf_op jit(solution)/shard_map/while/body/eval_jaxpr/dot_general | solution.py:45
  332.5 13.1 %pmax.52 = f32[96]{0:T(128)S(1)} all-reduce(f32[96]{0:T(128)S(1)} %abs_reduce_fusion.3), channel_id=1, replica_groups=mesh['segment'=4,'col'=8] {'col'}, use_global_device_ids=true, to_apply=%region_31.34 | all-reduce | flops 96 | bytes 768 | tf_op jit(solution)/shard_map/pmax | solution.py:50
  345.9 1.3 collective-permute-start.3
  347.2 6.5 %collective-permute-done.3 = bf16[96,1024]{1,0:T(8,128)(2,1)S(1)} collective-permute-done((bf16[96,1024]{1,0:T(8,128)(2,1)S(1)}, bf16[96,1024]{1,0:T(8,128)(2,1)S(1)}, u32[]{:S(2)}, u32[]{:S(2)}) %collective-permute-start.3) | collective-permute-done | bytes 196640 | tf_op jit(solution)/shard_map/ppermute | solution.py:15
  358.7 34.9 %all-gather.16.cloned.1.call-done = bf16[192,8192]{1,0:T(8,128)(2,1)} async-done(((bf16[192,1024]{1,0:T(8,128)(2,1)}), bf16[192,8192]{1,0:T(8,128)(2,1)}) %all-gather.16.cloned.1.call-update) | async-done | bytes 3145744 | tf_op jit(solution)/shard_map/all_gather | solution.py:36
  393.7 23.1 %while.74 = (s32[]{:T(128)}, f32[2,96,1024]{2,1,0:T(8,128)S(1)}, bf16[2,96,8192]{2,1,0:T(8,128)(2,1)}, s32[2]{0:T(128)S(1)}, bf16[2,8192,1024]{2,1,0:T(8,128)(2,1)}, /*index=5*/s32[]{:T(128)}, s32[]{:T(128)}, s32[]{:T(128)}) while((s32[]{:T(128)}, f32[2,96,1024]{2,1,0:T(8,128)S(1)}, bf16[2,96,8192]{2,1,0:T(8,128)(2,1)}, s32[2]{0:T(128)S(1)}, ...), condition=%wide.region_37.40_spmd, body=%wide.region_36.39_spmd.sunk | while | flops 1610612736 | bytes 18744456 | solution.py:47
  396.2 9.0 %fusion.204 = f32[2,96,1024]{2,1,0:T(8,128)S(1)} fusion(f32[2,96,1024]{2,1,0:T(8,128)S(1)} %get-tuple-element.678, s32[]{:T(128)} %get-tuple-element.677, bf16[2,8192,1024]{2,1,0:T(8,128)(2,1)} %get-tuple-element.689, s32[]{:T(128)S(6)} %select_n.657, bf16[2,96,8192]{2,1,0:T(8,128)(2,1)} %get-tuple-element.687), kind=kOutput, calls=%fused_computation.66.clone.1 | convolution fusion | flops 1610612736 | bytes 18744324 | tf_op jit(solution)/shard_map/while/body/eval_jaxpr/dot_general | solution.py:45
  407.8 9.0 %fusion.204 = f32[2,96,1024]{2,1,0:T(8,128)S(1)} fusion(f32[2,96,1024]{2,1,0:T(8,128)S(1)} %get-tuple-element.678, s32[]{:T(128)} %get-tuple-element.677, bf16[2,8192,1024]{2,1,0:T(8,128)(2,1)} %get-tuple-element.689, s32[]{:T(128)S(6)} %select_n.657, bf16[2,96,8192]{2,1,0:T(8,128)(2,1)} %get-tuple-element.687), kind=kOutput, calls=%fused_computation.66.clone.1 | convolution fusion | flops 1610612736 | bytes 18744324 | tf_op jit(solution)/shard_map/while/body/eval_jaxpr/dot_general | solution.py:45
  417.8 13.1 %pmax.53 = f32[96]{0:T(128)S(1)} all-reduce(f32[96]{0:T(128)S(1)} %abs_reduce_fusion.2), channel_id=1, replica_groups=mesh['segment'=4,'col'=8] {'col'}, use_global_device_ids=true, to_apply=%region_39.42 | all-reduce | flops 96 | bytes 768 | tf_op jit(solution)/shard_map/pmax | solution.py:50
  431.1 1.3 collective-permute-start.4
  432.4 6.5 %collective-permute-done.4 = bf16[96,1024]{1,0:T(8,128)(2,1)S(1)} collective-permute-done((bf16[96,1024]{1,0:T(8,128)(2,1)S(1)}, bf16[96,1024]{1,0:T(8,128)(2,1)S(1)}, u32[]{:S(2)}, u32[]{:S(2)}) %collective-permute-start.4) | collective-permute-done | bytes 196640 | tf_op jit(solution)/shard_map/ppermute | solution.py:15
  443.9 34.9 %all-gather.18.cloned.1.call-done = bf16[192,8192]{1,0:T(8,128)(2,1)} async-done(((bf16[192,1024]{1,0:T(8,128)(2,1)}), bf16[192,8192]{1,0:T(8,128)(2,1)}) %all-gather.18.cloned.1.call-update) | async-done | bytes 3145744 | tf_op jit(solution)/shard_map/all_gather | solution.py:36
  478.9 23.1 %while.75 = (s32[]{:T(128)}, f32[2,96,1024]{2,1,0:T(8,128)S(1)}, bf16[2,96,8192]{2,1,0:T(8,128)(2,1)}, s32[2]{0:T(128)S(1)}, bf16[2,8192,1024]{2,1,0:T(8,128)(2,1)}, /*index=5*/s32[]{:T(128)}, s32[]{:T(128)}, s32[]{:T(128)}) while((s32[]{:T(128)}, f32[2,96,1024]{2,1,0:T(8,128)S(1)}, bf16[2,96,8192]{2,1,0:T(8,128)(2,1)}, s32[2]{0:T(128)S(1)}, ...), condition=%wide.region_45.48_spmd, body=%wide.region_44.47_spmd.sunk | while | flops 1610612736 | bytes 18744456 | solution.py:47
  481.5 9.0 %fusion.207 = f32[2,96,1024]{2,1,0:T(8,128)S(1)} fusion(f32[2,96,1024]{2,1,0:T(8,128)S(1)} %get-tuple-element.702, s32[]{:T(128)} %get-tuple-element.701, bf16[2,8192,1024]{2,1,0:T(8,128)(2,1)} %get-tuple-element.713, s32[]{:T(128)S(6)} %select_n.658, bf16[2,96,8192]{2,1,0:T(8,128)(2,1)} %get-tuple-element.711), kind=kOutput, calls=%fused_computation.74.clone.1 | convolution fusion | flops 1610612736 | bytes 18744324 | tf_op jit(solution)/shard_map/while/body/eval_jaxpr/dot_general | solution.py:45
  493.1 9.0 %fusion.207 = f32[2,96,1024]{2,1,0:T(8,128)S(1)} fusion(f32[2,96,1024]{2,1,0:T(8,128)S(1)} %get-tuple-element.702, s32[]{:T(128)} %get-tuple-element.701, bf16[2,8192,1024]{2,1,0:T(8,128)(2,1)} %get-tuple-element.713, s32[]{:T(128)S(6)} %select_n.658, bf16[2,96,8192]{2,1,0:T(8,128)(2,1)} %get-tuple-element.711), kind=kOutput, calls=%fused_computation.74.clone.1 | convolution fusion | flops 1610612736 | bytes 18744324 | tf_op jit(solution)/shard_map/while/body/eval_jaxpr/dot_general | solution.py:45
  503.0 13.1 %pmax.54 = f32[96]{0:T(128)S(1)} all-reduce(f32[96]{0:T(128)S(1)} %abs_reduce_fusion.1), channel_id=1, replica_groups=mesh['segment'=4,'col'=8] {'col'}, use_global_device_ids=true, to_apply=%region_47.50 | all-reduce | flops 96 | bytes 768 | tf_op jit(solution)/shard_map/pmax | solution.py:50
  516.4 1.3 collective-permute-start.5
  517.7 6.5 %collective-permute-done.5 = bf16[96,1024]{1,0:T(8,128)(2,1)S(1)} collective-permute-done((bf16[96,1024]{1,0:T(8,128)(2,1)S(1)}, bf16[96,1024]{1,0:T(8,128)(2,1)S(1)}, u32[]{:S(2)}, u32[]{:S(2)}) %collective-permute-start.5) | collective-permute-done | bytes 196640 | tf_op jit(solution)/shard_map/ppermute | solution.py:15
  526.2 37.9 %all-gather.20.cloned.1.call-done = bf16[192,8192]{1,0:T(8,128)(2,1)} async-done(((bf16[192,1024]{1,0:T(8,128)(2,1)}), bf16[192,8192]{1,0:T(8,128)(2,1)}) %all-gather.20.cloned.1.call-update) | async-done | bytes 3145744 | tf_op jit(solution)/shard_map/all_gather | solution.py:36
  564.2 23.1 %while.76 = (s32[]{:T(128)}, f32[2,96,1024]{2,1,0:T(8,128)S(1)}, bf16[2,96,8192]{2,1,0:T(8,128)(2,1)}, s32[2]{0:T(128)S(1)}, bf16[2,8192,1024]{2,1,0:T(8,128)(2,1)}, /*index=5*/s32[]{:T(128)}, s32[]{:T(128)}, s32[]{:T(128)}) while((s32[]{:T(128)}, f32[2,96,1024]{2,1,0:T(8,128)S(1)}, bf16[2,96,8192]{2,1,0:T(8,128)(2,1)}, s32[2]{0:T(128)S(1)}, ...), condition=%wide.region_53.56_spmd, body=%wide.region_52.55_spmd.sunk | while | flops 1610612736 | bytes 18744456 | solution.py:47
  566.8 9.0 %fusion.210 = f32[2,96,1024]{2,1,0:T(8,128)S(1)} fusion(f32[2,96,1024]{2,1,0:T(8,128)S(1)} %get-tuple-element.726, s32[]{:T(128)} %get-tuple-element.725, bf16[2,8192,1024]{2,1,0:T(8,128)(2,1)} %get-tuple-element.737, s32[]{:T(128)S(6)} %select_n.659, bf16[2,96,8192]{2,1,0:T(8,128)(2,1)} %get-tuple-element.735), kind=kOutput, calls=%fused_computation.82.clone.1 | convolution fusion | flops 1610612736 | bytes 18744324 | tf_op jit(solution)/shard_map/while/body/eval_jaxpr/dot_general | solution.py:45
  578.3 9.0 %fusion.210 = f32[2,96,1024]{2,1,0:T(8,128)S(1)} fusion(f32[2,96,1024]{2,1,0:T(8,128)S(1)} %get-tuple-element.726, s32[]{:T(128)} %get-tuple-element.725, bf16[2,8192,1024]{2,1,0:T(8,128)(2,1)} %get-tuple-element.737, s32[]{:T(128)S(6)} %select_n.659, bf16[2,96,8192]{2,1,0:T(8,128)(2,1)} %get-tuple-element.735), kind=kOutput, calls=%fused_computation.82.clone.1 | convolution fusion | flops 1610612736 | bytes 18744324 | tf_op jit(solution)/shard_map/while/body/eval_jaxpr/dot_general | solution.py:45
  588.3 13.1 %pmax.55 = f32[96]{0:T(128)S(1)} all-reduce(f32[96]{0:T(128)S(1)} %abs_reduce_fusion), channel_id=1, replica_groups=mesh['segment'=4,'col'=8] {'col'}, use_global_device_ids=true, to_apply=%region_55.58 | all-reduce | flops 96 | bytes 768 | tf_op jit(solution)/shard_map/pmax | solution.py:50
  (184 shorter events, 49.9 us)
Async XLA Ops:
  7.2 45.3 %all-gather.8.cloned.1.call-start = ((), (), s32[]{:S(2)}) async-start(), calls=%async_computation | async-start | bytes 3538944 | tf_op jit(solution)/shard_map/all_gather | solution.py:36
  14.8 123.0 %all-gather.10.cloned.1.call-start = ((), (), s32[]{:S(2)}) async-start(), calls=%async_computation.1 | async-start | bytes 3538944 | tf_op jit(solution)/shard_map/all_gather | solution.py:36
  75.7 22.1 %copy-start = (bf16[384,1024]{1,0:T(8,128)(2,1)S(1)}, bf16[384,1024]{1,0:T(8,128)(2,1)}, u32[]{:S(2)}) copy-start(bf16[384,1024]{1,0:T(8,128)(2,1)} %param.21) | copy-start | bytes 2359300
  90.0 7.8 %collective-permute-start = (bf16[96,1024]{1,0:T(8,128)(2,1)S(1)}, bf16[96,1024]{1,0:T(8,128)(2,1)S(1)}, u32[]{:S(2)}, u32[]{:S(2)}) collective-permute-start(bf16[96,1024]{1,0:T(8,128)(2,1)S(1)} %get-tuple-element.319), channel_id=1, source_target_pairs={{0,8},{8,16},{16,24},{1,9},{9,17},{17,25},{2,10},{10,18},{18,26},{... | collective-permute-start | bytes 589832 | tf_op jit(solution)/shard_map/ppermute | solution.py:15
  99.8 123.3 %all-gather.12.cloned.1.call-start = ((), (), s32[]{:S(2)}) async-start(), calls=%async_computation.2 | async-start | bytes 3538944 | tf_op jit(solution)/shard_map/all_gather | solution.py:36
  175.3 7.8 %collective-permute-start.1 = (bf16[96,1024]{1,0:T(8,128)(2,1)S(1)}, bf16[96,1024]{1,0:T(8,128)(2,1)S(1)}, u32[]{:S(2)}, u32[]{:S(2)}) collective-permute-start(bf16[96,1024]{1,0:T(8,128)(2,1)S(1)} %get-tuple-element.313), channel_id=1, source_target_pairs={{0,8},{8,16},{16,24},{1,9},{9,17},{17,25},{2,10},{10,18},{18,26},{... | collective-permute-start | bytes 589832 | tf_op jit(solution)/shard_map/ppermute | solution.py:15
  185.0 123.3 %all-gather.14.cloned.1.call-start = ((), (), s32[]{:S(2)}) async-start(), calls=%async_computation.3 | async-start | bytes 3538944 | tf_op jit(solution)/shard_map/all_gather | solution.py:36
  260.6 7.8 %collective-permute-start.2 = (bf16[96,1024]{1,0:T(8,128)(2,1)S(1)}, bf16[96,1024]{1,0:T(8,128)(2,1)S(1)}, u32[]{:S(2)}, u32[]{:S(2)}) collective-permute-start(bf16[96,1024]{1,0:T(8,128)(2,1)S(1)} %get-tuple-element.307), channel_id=1, source_target_pairs={{0,8},{8,16},{16,24},{1,9},{9,17},{17,25},{2,10},{10,18},{18,26},{... | collective-permute-start | bytes 589832 | tf_op jit(solution)/shard_map/ppermute | solution.py:15
  270.3 123.3 %all-gather.16.cloned.1.call-start = ((), (), s32[]{:S(2)}) async-start(), calls=%async_computation.4 | async-start | bytes 3538944 | tf_op jit(solution)/shard_map/all_gather | solution.py:36
  345.9 7.8 %collective-permute-start.3 = (bf16[96,1024]{1,0:T(8,128)(2,1)S(1)}, bf16[96,1024]{1,0:T(8,128)(2,1)S(1)}, u32[]{:S(2)}, u32[]{:S(2)}) collective-permute-start(bf16[96,1024]{1,0:T(8,128)(2,1)S(1)} %get-tuple-element.301), channel_id=1, source_target_pairs={{0,8},{8,16},{16,24},{1,9},{9,17},{17,25},{2,10},{10,18},{18,26},{... | collective-permute-start | bytes 589832 | tf_op jit(solution)/shard_map/ppermute | solution.py:15
  355.6 123.3 %all-gather.18.cloned.1.call-start = ((), (), s32[]{:S(2)}) async-start(), calls=%async_computation.5 | async-start | bytes 3538944 | tf_op jit(solution)/shard_map/all_gather | solution.py:36
  431.1 7.8 %collective-permute-start.4 = (bf16[96,1024]{1,0:T(8,128)(2,1)S(1)}, bf16[96,1024]{1,0:T(8,128)(2,1)S(1)}, u32[]{:S(2)}, u32[]{:S(2)}) collective-permute-start(bf16[96,1024]{1,0:T(8,128)(2,1)S(1)} %get-tuple-element.295), channel_id=1, source_target_pairs={{0,8},{8,16},{16,24},{1,9},{9,17},{17,25},{2,10},{10,18},{18,26},{... | collective-permute-start | bytes 589832 | tf_op jit(solution)/shard_map/ppermute | solution.py:15
  440.9 123.3 %all-gather.20.cloned.1.call-start = ((), (), s32[]{:S(2)}) async-start(), calls=%async_computation.6 | async-start | bytes 3538944 | tf_op jit(solution)/shard_map/all_gather | solution.py:36
  516.4 7.8 %collective-permute-start.5 = (bf16[96,1024]{1,0:T(8,128)(2,1)S(1)}, bf16[96,1024]{1,0:T(8,128)(2,1)S(1)}, u32[]{:S(2)}, u32[]{:S(2)}) collective-permute-start(bf16[96,1024]{1,0:T(8,128)(2,1)S(1)} %get-tuple-element.289), channel_id=1, source_target_pairs={{0,8},{8,16},{16,24},{1,9},{9,17},{17,25},{2,10},{10,18},{18,26},{... | collective-permute-start | bytes 589832 | tf_op jit(solution)/shard_map/ppermute | solution.py:15
  601.6 0.6 copy-start.2
  602.2 0.9 copy-start.1
Sparse Core Ops, SparseCore 0:
  14.9 37.5 all-gather.7
  99.9 37.8 all-gather.9
  185.2 37.8 all-gather.11
  270.4 37.8 all-gather.13
  355.7 37.8 all-gather.15
  441.0 37.8 all-gather.17
  526.2 37.8 all-gather.19
where the time goes:
time: 616 us; the launch traced here: 610 us
  waiting for transfers between devices  286 us (46%)
  matrix products  126 us (20%)
  blocking collectives  91.4 us (15%)
  local copies, waits for them, and re-layouts  36 us (6%)
  loops' own time  27.4 us (4%)
  between operations  19.5 us (3%)
  other arithmetic  15.2 us (2%)
  starting transfers between devices  8.22 us (1%)
    all_gather x7, waiting for transfers between devices, advance(): gathered_piece = lax.all_gather(arranged_in, 'col', axis=1, tiled=True)  247 us
    dot_general x14, matrix products, one_block(): return jnp.dot(rows_block, weight_block, preferred_element_type=jnp.float32)  126 us
    pmax x7, blocking collectives, advance(): maximum = lax.pmax(jnp.max(jnp.abs(chosen), axis=1), 'col') + epsilon  91.4 us
    ppermute x6, waiting for transfers between devices, passed_along(): return lax.ppermute(value, axis, pairs)  38.5 us
    another operation x7, loops' own time, advance(): result = lax.map(one_block, (pieces, block_bit))  27.4 us
  transfers between devices with their start and end apart: 13, of which 13 were waited for; matrix products, arithmetic and copies ran while one was open for 2% of the time, Pallas kernels for 0%

commit v1 on v0

v1 whole, which is shorter than its diff:
```python
import functools

import jax
import jax.numpy as jnp
from jax import lax
from jax.experimental import pallas as pl
from jax.experimental.pallas import tpu as pltpu
from jax.sharding import PartitionSpec as P

GRANULES = 8
EPSILON = 1e-06
MESH = pl.DeviceIdType.MESH


def granules_of(rows):
    for count in range(GRANULES, 0, -1):
        if rows % count == 0 and (rows // count) % 16 == 0:
            return count
    return 1


def chip_at(step, z, n):
    below, above = z, n - 1 - z
    both = jnp.minimum(below, above)
    paired = (step + 1) // 2
    near = jnp.where(step % 2 == 1, z - paired, z + paired)
    far = jnp.where(below < above, z + (step - both), z - (step - both))
    return jnp.where(step <= 2 * both, near, far)


def kernel(
    stages, peers, granules,
    env_in, bits_in, tensor_in, env_out, log_out,
    weights, pieces, product, outgoing, peak, peak_sent, peak_all, scale_in, scale_sent,
    load_sem, weight_sem, arrive_sem, up_sem, down_sem, cross_sem, next_sem,
    peak_send_sem, peak_recv_sem, scale_send_sem, scale_recv_sem,
):
    rows, width = outgoing.shape
    block = rows // granules
    n = peers // 2
    stage = lax.axis_index("segment")
    me = lax.axis_index("col")
    z = me // 2
    core = me % 2

    def there(segment, col):
        return {"segment": segment, "col": col}

    load = pltpu.make_async_copy(env_in, pieces.at[me], load_sem)

    @pl.when(stage == 0)
    def _():
        load.start()

    def owner_at(step):
        chip = chip_at(step // 2, z, n)
        return chip, chip * 2 + jnp.where(step % 2 == 0, core, 1 - core)

    def weight_copy(owner):
        return pltpu.make_async_copy(
            tensor_in.at[0, :, pl.ds(pl.multiple_of(owner * width, width), width), :],
            weights.at[owner],
            weight_sem.at[owner],
        )

    def start_weight(step, carry):
        weight_copy(owner_at(step)[1]).start()
        return carry

    lax.fori_loop(0, peers, start_weight, 0)

    barrier = pltpu.get_barrier_semaphore()

    def greet(by, carry):
        pl.semaphore_signal(
            barrier, inc=1, device_id=there(stage, (me + by) % peers), device_id_type=MESH
        )
        return carry

    lax.fori_loop(1, peers, greet, 0)

    @pl.when(stage > 0)
    def _():
        pl.semaphore_signal(barrier, inc=1, device_id=there(stage - 1, me), device_id_type=MESH)

    @pl.when(stage < stages - 1)
    def _():
        pl.semaphore_signal(barrier, inc=1, device_id=there(stage + 1, me), device_id_type=MESH)

    neighbours = jnp.where(stage > 0, 1, 0) + jnp.where(stage < stages - 1, 1, 0)
    pl.semaphore_wait(barrier, peers - 1 + neighbours)

    @pl.when(stage == 0)
    def _():
        load.wait()

    def rows_of(granule):
        return pl.ds(pl.multiple_of(granule * block, block), block)

    def piece(granule, owner):
        return pieces.at[owner, rows_of(granule), :]

    def along(granule, owner, send, col):
        part = piece(granule, owner)
        return pltpu.make_async_remote_copy(
            src_ref=part,
            dst_ref=part,
            send_sem=send.at[granule, owner // 2],
            recv_sem=arrive_sem.at[granule, owner],
            device_id=there(stage, col),
            device_id_type=MESH,
        )

    def up(granule, owner):
        return along(granule, owner, up_sem, me + 2)

    def down(granule, owner):
        return along(granule, owner, down_sem, me - 2)

    def cross(granule, owner):
        return along(granule, owner, cross_sem, 2 * z + 1 - core)

    def onward(granule):
        return pltpu.make_async_remote_copy(
            src_ref=outgoing.at[rows_of(granule), :],
            dst_ref=piece(granule, me),
            send_sem=next_sem.at[granule],
            recv_sem=arrive_sem.at[granule, me],
            device_id=there(stage + 1, me),
            device_id_type=MESH,
        )

    def one_granule(granule, carry):
        bit = bits_in[rows_of(granule), :].astype(jnp.float32).astype(jnp.bfloat16)

        def one_piece(step, carry):
            chip, owner = owner_at(step)

            @pl.when((stage > 0) | (step > 0))
            def _():
                along(granule, owner, cross_sem, 2 * z + 1 - core).wait_recv()

            @pl.when(step % 2 == 0)
            def _():
                @pl.when((chip <= z) & (z < n - 1))
                def _():
                    up(granule, owner).start()

                @pl.when((chip >= z) & (z > 0))
                def _():
                    down(granule, owner).start()

                cross(granule, owner).start()

            @pl.when(granule == 0)
            def _():
                weight_copy(owner).wait()

            value = piece(granule, owner)[...]
            one = value * bit
            both = jnp.concatenate([value - one, one], axis=1)
            part = jnp.dot(
                both,
                weights[owner].reshape(2 * width, width),
                preferred_element_type=jnp.float32,
            )

            @pl.when(step == 0)
            def _():
                product[rows_of(granule), :] = part

            @pl.when(step > 0)
            def _():
                product[rows_of(granule), :] += part

            return carry

        lax.fori_loop(0, peers, one_piece, 0)
        done = product[rows_of(granule), :]
        outgoing[rows_of(granule), :] = done.astype(jnp.bfloat16)

        @pl.when(stage < stages - 1)
        def _():
            onward(granule).start()

        largest = jnp.max(jnp.abs(done), axis=1, keepdims=True)
        peak[rows_of(granule), :] = jnp.broadcast_to(largest, (block, peak.shape[1]))
        return carry

    lax.fori_loop(0, granules, one_granule, 0)

    mine = jnp.transpose(peak[...])[:8]
    peak_sent[...] = mine

    def peak_copy(by):
        return pltpu.make_async_remote_copy(
            src_ref=peak_sent,
            dst_ref=peak_all.at[by],
            send_sem=peak_send_sem.at[by],
            recv_sem=peak_recv_sem.at[by],
            device_id=there(stage, (me + by) % peers),
            device_id_type=MESH,
        )

    def start_peak(by, carry):
        peak_copy(by).start()
        return carry

    lax.fori_loop(1, peers, start_peak, 0)

    scale_copy = pltpu.make_async_remote_copy(
        src_ref=scale_sent,
        dst_ref=scale_in,
        send_sem=scale_send_sem,
        recv_sem=scale_recv_sem,
        device_id=there(stage + 1, me),
        device_id_type=MESH,
    )

    @pl.when(stage == 0)
    def _():
        scale_in[...] = jnp.ones_like(scale_in)

    @pl.when(stage > 0)
    def _():
        scale_copy.wait_recv()

    def take_peak(by, largest):
        peak_copy(by).wait_recv()
        return jnp.maximum(largest, peak_all[by])

    largest = lax.fori_loop(1, peers, take_peak, mine)
    before = scale_in[...]
    scale = largest + EPSILON * before
    scale_sent[...] = scale

    @pl.when(stage < stages - 1)
    def _():
        scale_copy.start()

    log_out[...] = jnp.log(largest / before + EPSILON)[:1]
    by_row = jnp.transpose(jnp.broadcast_to(scale[:1], (128, rows)))[:, :1]
    env_out[0] = (product[...] / by_row).astype(jnp.bfloat16)

    def drain(granule, carry):
        def drain_chip(chip, carry):
            owner = chip * 2 + core

            @pl.when((chip <= z) & (z < n - 1))
            def _():
                up(granule, owner).wait_send()

            @pl.when((chip >= z) & (z > 0))
            def _():
                down(granule, owner).wait_send()

            cross(granule, owner).wait_send()
            return carry

        lax.fori_loop(0, n, drain_chip, 0)

        @pl.when(stage < stages - 1)
        def _():
            onward(granule).wait_send()

        return carry

    lax.fori_loop(0, granules, drain, 0)

    def drain_peak(by, carry):
        peak_copy(by).wait_send()
        return carry

    lax.fori_loop(1, peers, drain_peak, 0)

    @pl.when(stage < stages - 1)
    def _():
        scale_copy.wait_send()


def solution(mesh):
    stages, peers = mesh.shape["segment"], mesh.shape["col"]
    n = peers // 2

    def local(left_env, bit_strings, site_tensors):
        rows, width = left_env.shape
        granules = granules_of(rows)
        vmem = pl.BlockSpec(memory_space=pltpu.VMEM)
        anywhere = pl.BlockSpec(memory_space=pl.ANY)
        dma = pltpu.SemaphoreType.DMA
        return pl.pallas_call(
            functools.partial(kernel, stages, peers, granules),
            out_shape=(
                jax.ShapeDtypeStruct((1, rows, width), jnp.bfloat16),
                jax.ShapeDtypeStruct((1, rows), jnp.float32),
            ),
            in_specs=[anywhere, vmem, anywhere],
            out_specs=(vmem, vmem),
            scratch_shapes=[
                pltpu.VMEM((peers, 2, width, width), jnp.bfloat16),
                pltpu.VMEM((peers, rows, width), jnp.bfloat16),
                pltpu.VMEM((rows, width), jnp.float32),
                pltpu.VMEM((rows, width), jnp.bfloat16),
                pltpu.VMEM((rows, 128), jnp.float32),
                pltpu.VMEM((8, rows), jnp.float32),
                pltpu.VMEM((peers, 8, rows), jnp.float32),
                pltpu.VMEM((8, rows), jnp.float32),
                pltpu.VMEM((8, rows), jnp.float32),
                dma,
                dma((peers,)),
                dma((granules, peers)),
                dma((granules, n)),
                dma((granules, n)),
                dma((granules, n)),
                dma((granules,)),
                dma((peers,)),
                dma((peers,)),
                dma,
                dma,
            ],
            compiler_params=pltpu.CompilerParams(
                collective_id=0, has_side_effects=True, vmem_limit_bytes=60 * 1024 * 1024
            ),
        )(left_env, bit_strings, site_tensors)

    return jax.shard_map(
        local,
        mesh=mesh,
        in_specs=(P(None, "col"), P(None, "segment"), P("segment", None, None, "col")),
        out_specs=(P("segment", None, "col"), P("segment", None)),
        check_vma=False,
    )
```

time: 616 us -> 190 us (0.31)
  waiting for transfers between devices: 286 us -> 0 us
  Pallas kernels: 0 us -> 184 us
  matrix products: 126 us -> 0 us
  blocking collectives: 91.4 us -> 0 us
  local copies, waits for them, and re-layouts: 36 us -> 4.8 us
  loops' own time: 27.4 us -> 0 us
  between operations: 19.5 us -> 0.64 us
  other arithmetic: 15.2 us -> 0 us
  starting transfers between devices: 8.22 us -> 0 us
    all_gather x7 -> x0, waiting for transfers between devices: 247 us -> none  [advance(): gathered_piece = lax.all_gather(arranged_in, 'col', axis=1, tiled=True)]
    pallas_call x0 -> x1, Pallas kernels: none -> 184 us  [local(): pl.pallas_call(functools.partial(kernel, stages, peers, granules), out_sh...]
    dot_general x14 -> x0, matrix products: 126 us -> none  [one_block(): return jnp.dot(rows_block, weight_block, preferred_element_type=jnp.float32)]
    pmax x7 -> x0, blocking collectives: 91.4 us -> none  [advance(): maximum = lax.pmax(jnp.max(jnp.abs(chosen), axis=1), 'col') + epsilon]
    ppermute x6 -> x0, waiting for transfers between devices: 38.5 us -> none  [passed_along(): return lax.ppermute(value, axis, pairs)]
    another operation x7 -> x0, loops' own time: 27.4 us -> none  [advance(): result = lax.map(one_block, (pieces, block_bit))]
    scatter x14 -> x0, local copies, waits for them, and re-layouts: 12.6 us -> none  [the longest x7 6.34 us: advance(): source = jnp.zeros((buffer_rows,), jnp.int32).at[slot].set(index_rows)]
    gather x14 -> x0, local copies, waits for them, and re-layouts: 12.3 us -> none  [the longest x7 7.12 us: advance(): jnp.take(vector, source, axis=0)]
  transfers between devices with their start and end apart: 13 -> 0, of which waited for: 13 -> 0; matrix products, arithmetic and copies ran while one was open for 2% -> 0% of each run, Pallas kernels for 0% -> 0%
where the time goes in v1:
time: 190 us
  Pallas kernels  184 us (97%)
  local copies, waits for them, and re-layouts  4.8 us (3%)
    pallas_call x1, Pallas kernels, local(): pl.pallas_call(functools.partial(kernel, stages, peers, granules), out_sh...  184 us
    unnamed x3, local copies, waits for them, and re-layouts  4.8 us

profile of v1, /device:TPU:31, one launch (start us, length us, event | category | flops | bytes accessed | tf_op | source)
XLA Modules:
  0.0 189.7 jit_solution(13883909601228938211)
XLA Ops:
  0.6 1.5 copy.5.bits_in
  2.1 184.3 %shard_map.50 = (bf16[1,384,1024]{2,1,0:T(8,128)(2,1)}, f32[1,384]{1,0:T(1,128)}) custom-call(bf16[384,1024]{1,0:T(8,128)(2,1)} %env_in.1, s32[384,1]{1,0:T(8,128)} %copy.5.bits_in, bf16[1,2,8192,1024]{3,2,1,0:T(8,128)(2,1)} %tensor_in.1), custom_call_target="tpu_custom_call" | custom-call | tf_op jit(solution)/shard_map/pallas_call | solution.py:291
  186.4 2.1 %copy.8 = bf16[1,384,1024]{2,1,0:T(8,128)(2,1)} copy(bf16[1,384,1024]{2,1,0:T(8,128)(2,1)} %get-tuple-element.4) | data formatting | bytes 1572864
  188.5 1.2 copy.9

commit v2 on v1

--- a/solution.py
+++ b/solution.py
@@ -7,7 +7,8 @@
 from jax.experimental.pallas import tpu as pltpu
 from jax.sharding import PartitionSpec as P
 
-GRANULES = 8
+GRANULES = 12
+DIRECT = True
 EPSILON = 1e-06
 MESH = pl.DeviceIdType.MESH
 
@@ -32,7 +33,7 @@
     stages, peers, granules,
     env_in, bits_in, tensor_in, env_out, log_out,
     weights, pieces, product, outgoing, peak, peak_sent, peak_all, scale_in, scale_sent,
-    load_sem, weight_sem, arrive_sem, up_sem, down_sem, cross_sem, next_sem,
+    load_sem, weight_sem, arrive_sem, line_sem, cross_sem, next_sem,
     peak_send_sem, peak_recv_sem, scale_send_sem, scale_recv_sem,
 ):
     rows, width = outgoing.shape
@@ -53,8 +54,8 @@
         load.start()
 
     def owner_at(step):
-        chip = chip_at(step // 2, z, n)
-        return chip, chip * 2 + jnp.where(step % 2 == 0, core, 1 - core)
+        chip = chip_at(step % n, z, n)
+        return chip, chip * 2 + jnp.where(step < n, core, 1 - core)
 
     def weight_copy(owner):
         return pltpu.make_async_copy(
@@ -79,16 +80,23 @@
 
     lax.fori_loop(1, peers, greet, 0)
 
-    @pl.when(stage > 0)
-    def _():
-        pl.semaphore_signal(barrier, inc=1, device_id=there(stage - 1, me), device_id_type=MESH)
-
-    @pl.when(stage < stages - 1)
-    def _():
-        pl.semaphore_signal(barrier, inc=1, device_id=there(stage + 1, me), device_id_type=MESH)
-
-    neighbours = jnp.where(stage > 0, 1, 0) + jnp.where(stage < stages - 1, 1, 0)
-    pl.semaphore_wait(barrier, peers - 1 + neighbours)
+    count = jnp.int32(0)
+    for by in (-2, -1, 0, 1, 2):
+        inside = (z + by >= 0) & (z + by < n)
+        for other in (-1, 1):
+            meets = inside & (stage + other >= 0) & (stage + other < stages)
+
+            @pl.when(meets)
+            def _():
+                pl.semaphore_signal(
+                    barrier,
+                    inc=1,
+                    device_id=there(stage + other, me + 2 * by),
+                    device_id_type=MESH,
+                )
+
+            count = count + jnp.where(meets, 1, 0)
+    pl.semaphore_wait(barrier, peers - 1 + count)
 
     @pl.when(stage == 0)
     def _():
@@ -100,37 +108,63 @@
     def piece(granule, owner):
         return pieces.at[owner, rows_of(granule), :]
 
-    def along(granule, owner, send, col):
-        part = piece(granule, owner)
+    def send(source, granule, owner, sem, segment, col):
         return pltpu.make_async_remote_copy(
-            src_ref=part,
-            dst_ref=part,
-            send_sem=send.at[granule, owner // 2],
+            src_ref=source,
+            dst_ref=piece(granule, owner),
+            send_sem=sem,
             recv_sem=arrive_sem.at[granule, owner],
-            device_id=there(stage, col),
+            device_id=there(segment, col),
             device_id_type=MESH,
         )
 
-    def up(granule, owner):
-        return along(granule, owner, up_sem, me + 2)
-
-    def down(granule, owner):
-        return along(granule, owner, down_sem, me - 2)
-
     def cross(granule, owner):
-        return along(granule, owner, cross_sem, 2 * z + 1 - core)
-
-    def onward(granule):
-        return pltpu.make_async_remote_copy(
-            src_ref=outgoing.at[rows_of(granule), :],
-            dst_ref=piece(granule, me),
-            send_sem=next_sem.at[granule],
-            recv_sem=arrive_sem.at[granule, me],
-            device_id=there(stage + 1, me),
-            device_id_type=MESH,
-        )
+        col = 2 * z + 1 - core
+        return send(
+            piece(granule, owner), granule, owner, cross_sem.at[granule, owner // 2], stage, col
+        )
+
+    def along(act, granule, chip):
+        owner = chip * 2 + core
+        source = piece(granule, owner)
+        for slot, by in enumerate((1, -1, 2, -2)):
+            ahead = chip <= z if by > 0 else chip >= z
+            if DIRECT:
+                ahead = ahead & ((chip != z) | (stage == 0))
+
+            @pl.when(ahead & ((z - chip) % 2 == 0) & (z + by >= 0) & (z + by < n))
+            def _():
+                sem = line_sem.at[slot, granule, chip]
+                act(send(source, granule, owner, sem, stage, me + 2 * by))
+
+    def onward(act, granule):
+        source = outgoing.at[rows_of(granule), :]
+        for slot, by in enumerate((0, 1, -1, 2, -2) if DIRECT else (0,)):
+
+            @pl.when((stage < stages - 1) & (z + by >= 0) & (z + by < n))
+            def _():
+                sem = next_sem.at[slot, granule]
+                act(send(source, granule, me, sem, stage + 1, me + 2 * by))
+
+    def start(copy):
+        copy.start()
+
+    def sent(copy):
+        copy.wait_send()
+
+    def open_granule(granule):
+        @pl.when(stage == 0)
+        def _():
+            along(start, granule, z)
+            cross(granule, me).start()
+
+    open_granule(0)
 
     def one_granule(granule, carry):
+        @pl.when(granule + 1 < granules)
+        def _():
+            open_granule(granule + 1)
+
         bit = bits_in[rows_of(granule), :].astype(jnp.float32).astype(jnp.bfloat16)
 
         def one_piece(step, carry):
@@ -138,19 +172,12 @@
 
             @pl.when((stage > 0) | (step > 0))
             def _():
-                along(granule, owner, cross_sem, 2 * z + 1 - core).wait_recv()
-
-            @pl.when(step % 2 == 0)
-            def _():
-                @pl.when((chip <= z) & (z < n - 1))
+                cross(granule, owner).wait_recv()
+
+                @pl.when(step < n)
                 def _():
-                    up(granule, owner).start()
-
-                @pl.when((chip >= z) & (z > 0))
-                def _():
-                    down(granule, owner).start()
-
-                cross(granule, owner).start()
+                    along(start, granule, chip)
+                    cross(granule, owner).start()
 
             @pl.when(granule == 0)
             def _():
@@ -179,9 +206,7 @@
         done = product[rows_of(granule), :]
         outgoing[rows_of(granule), :] = done.astype(jnp.bfloat16)
 
-        @pl.when(stage < stages - 1)
-        def _():
-            onward(granule).start()
+        onward(start, granule)
 
         largest = jnp.max(jnp.abs(done), axis=1, keepdims=True)
         peak[rows_of(granule), :] = jnp.broadcast_to(largest, (block, peak.shape[1]))
@@ -244,25 +269,12 @@
 
     def drain(granule, carry):
         def drain_chip(chip, carry):
-            owner = chip * 2 + core
-
-            @pl.when((chip <= z) & (z < n - 1))
-            def _():
-                up(granule, owner).wait_send()
-
-            @pl.when((chip >= z) & (z > 0))
-            def _():
-                down(granule, owner).wait_send()
-
-            cross(granule, owner).wait_send()
+            along(sent, granule, chip)
+            cross(granule, chip * 2 + core).wait_send()
             return carry
 
         lax.fori_loop(0, n, drain_chip, 0)
-
-        @pl.when(stage < stages - 1)
-        def _():
-            onward(granule).wait_send()
-
+        onward(sent, granule)
         return carry
 
     lax.fori_loop(0, granules, drain, 0)
@@ -309,10 +321,9 @@
                 dma,
                 dma((peers,)),
                 dma((granules, peers)),
+                dma((4, granules, n)),
                 dma((granules, n)),
-                dma((granules, n)),
-                dma((granules, n)),
-                dma((granules,)),
+                dma((5, granules)),
                 dma((peers,)),
                 dma((peers,)),
                 dma,

time: 190 us -> 166 us (0.87)
  Pallas kernels: 184 us -> 161 us
    pallas_call x1, Pallas kernels: 184 us -> 161 us  [local(): pl.pallas_call(functools.partial(kernel, stages, peers, granules), out_sh...]
where the time goes in v2:
time: 166 us
  Pallas kernels  161 us (97%)
  local copies, waits for them, and re-layouts  4.8 us (3%)
    pallas_call x1, Pallas kernels, local(): pl.pallas_call(functools.partial(kernel, stages, peers, granules), out_sh...  161 us
    unnamed x3, local copies, waits for them, and re-layouts  4.8 us

profile of v2, /device:TPU:31, one launch (start us, length us, event | category | flops | bytes accessed | tf_op | source)
XLA Modules:
  0.0 166.2 jit_solution(4521324512477918634)
XLA Ops:
  0.6 1.5 copy.5.bits_in
  2.1 160.8 %shard_map.50 = (bf16[1,384,1024]{2,1,0:T(8,128)(2,1)}, f32[1,384]{1,0:T(1,128)}) custom-call(bf16[384,1024]{1,0:T(8,128)(2,1)} %env_in.1, s32[384,1]{1,0:T(8,128)} %copy.5.bits_in, bf16[1,2,8192,1024]{3,2,1,0:T(8,128)(2,1)} %tensor_in.1), custom_call_target="tpu_custom_call" | custom-call | tf_op jit(solution)/shard_map/pallas_call | solution.py:303
  162.9 2.1 %copy.8 = bf16[1,384,1024]{2,1,0:T(8,128)(2,1)} copy(bf16[1,384,1024]{2,1,0:T(8,128)(2,1)} %get-tuple-element.4) | data formatting | bytes 1572864
  165.0 1.2 copy.9
